TPU v7x, 32 devices: a whole 2x2x4 slice. The times are simulated.
32 devices in a mesh: gx: 2 (over core), gy: 4 (over y, x), gz: 4 (over z).
Axes of the slice: x: 2, y: 2, z: 4, core: 2. Of those that a mesh axis runs over, the one named last changes fastest.
Arguments:
- flexibility: bfloat16 [4, 4, 4, 1536, 1536], P('gx', 'gy', 'gz'), may hold values from -3 to 3, as said below
- dual_load: float32 [4, 4, 4, 3, 256, 128], P('gx', 'gy', 'gz'), may hold values from -20 to 20
- coarse_load: float32 [4, 4, 4, 128], replicated, may hold values from -384 to 384
- glue: int32 [4, 4, 4, 3], replicated, may hold values 0 or 1
- floating_flag: int32 [4, 4, 4], replicated, may hold values 0 or 1
Outputs:
- multipliers: float32 [4, 4, 4, 3, 256, 128], P('gx', 'gy', 'gz')
- residual: float32 [4, 4, 4, 3, 256, 128], P('gx', 'gy', 'gz')
Inputs may be any that keep to these rules, and one draw needn't show every extreme that they name: `flexibility`: for every subdomain the [1536, 1536] matrix is symmetric and positive definite.
All inputs are finite; a program needn't handle non-finite values.
Results may differ from a plain program's by a relative error of at most 0.015.
Values sent between devices are 32-bit elements; how exact they have to be, the bound alone decides.
A program may use at most 128 MiB of HBM per device.

v0:
```python
import math
import jax
import jax.numpy as jnp
from jax import lax
from jax.sharding import PartitionSpec as P

ITERS = 4


def padded_2(cells, sides, width):
    for axis, dim in sides:
        count = lax.axis_size(axis)
        ends = count - 1
        head = lax.slice_in_dim(cells, 0, width, axis=dim)
        tail = lax.slice_in_dim(cells, cells.shape[dim] - width, cells.shape[dim], axis=dim)
        cells = jnp.concatenate(
            [
                lax.ppermute(tail, axis, [(i, (i + 1) % count) for i in range(ends)]),
                cells,
                lax.ppermute(head, axis, [((i + 1) % count, i) for i in range(ends)]),
            ],
            axis=dim,
        )
    return cells


def shifted(values, dimension, toward):
    length = values.shape[dimension]
    widths = [(0, 0)] * values.ndim
    if toward > 0:
        widths[dimension] = (0, 1)
        return lax.slice_in_dim(jnp.pad(values, widths), 1, length + 1, axis=dimension)
    widths[dimension] = (1, 0)
    return lax.slice_in_dim(jnp.pad(values, widths), 0, length, axis=dimension)


def coupling(glue, floating_flag):
    grid_shape = floating_flag.shape
    active = []
    for dimension in range(3):
        coordinate = lax.broadcasted_iota(jnp.int32, grid_shape, dimension)
        inside = (coordinate < grid_shape[dimension] - 1).astype(jnp.int32)
        active.append(inside * glue[..., dimension])
    return (jnp.stack(active, axis=-1), floating_flag)


def coarse_matrix(active, floating):
    grid_shape = floating.shape
    total_count = grid_shape[0] * grid_shape[1] * grid_shape[2]
    strides = (grid_shape[1] * grid_shape[2], grid_shape[2], 1)
    support = 2.0 / float(grid_shape[0] * grid_shape[0])
    degree = jnp.zeros(grid_shape, jnp.int32)
    for dimension in range(3):
        degree = degree + active[..., dimension] + shifted(active[..., dimension], dimension, -1)
    flat_float = floating.reshape(total_count).astype(jnp.float32)
    diagonal = jnp.where(
        flat_float > 0, degree.reshape(total_count).astype(jnp.float32) + support, 1.0
    )
    row_index = lax.broadcasted_iota(jnp.int32, (total_count, total_count), 0)
    col_index = lax.broadcasted_iota(jnp.int32, (total_count, total_count), 1)
    matrix = jnp.where(row_index == col_index, diagonal[:, None], 0.0)
    for dimension in range(3):
        link_weight = (
            (active[..., dimension] * floating * shifted(floating, dimension, 1))
            .reshape(total_count)
            .astype(jnp.float32)
        )
        upper_band = jnp.where(
            col_index == row_index + strides[dimension], link_weight[:, None], 0.0
        )
        matrix = matrix - upper_band - upper_band.T
    return matrix


def alternate(low_part, high_part, dimension):
    joined = jnp.stack([low_part, high_part], axis=dimension + 1)
    new_shape = (
        low_part.shape[:dimension]
        + (2 * low_part.shape[dimension],)
        + low_part.shape[dimension + 1 :]
    )
    return joined.reshape(new_shape)


def separate(padded, dimension, layers):
    from_above = lax.slice_in_dim(padded, 3, 2 * layers + 2, stride=2, axis=dimension)
    from_below = lax.slice_in_dim(padded, 0, 2 * layers, stride=2, axis=dimension)
    return (from_above, from_below)


def per_device(flexibility, dual_load, coarse_load, glue, floating_flag):
    block_x, block_y, block_z = (dual_load.shape[0], dual_load.shape[1], dual_load.shape[2])
    face_dofs, cases = (dual_load.shape[4], dual_load.shape[5])
    grid_x, grid_y, grid_z = floating_flag.shape
    subdomains = grid_x * grid_y * grid_z
    local_count = block_x * block_y * block_z
    start_x = lax.axis_index("gx") * block_x
    start_y = lax.axis_index("gy") * block_y
    start_z = lax.axis_index("gz") * block_z
    active_int, floating_int = coupling(glue, floating_flag)
    factor = jnp.linalg.cholesky(coarse_matrix(active_int, floating_int))
    mode_value = 1.0 / math.sqrt(face_dofs)
    support_value = 2.0 / float(grid_x * grid_x)
    active_global = active_int.astype(jnp.float32)
    below_global = jnp.stack(
        [shifted(active_global[..., dimension], dimension, -1) for dimension in range(3)], axis=-1
    )
    floating_global = floating_int.astype(jnp.float32)
    full_shape = (block_x, block_y, block_z, 3, face_dofs, cases)

    def own_block(values):
        return lax.dynamic_slice(
            values,
            (start_x, start_y, start_z) + (0,) * (values.ndim - 3),
            (block_x, block_y, block_z) + values.shape[3:],
        )

    upper_active = own_block(active_global)
    lower_active = own_block(below_global)
    upper_mask = upper_active[..., None, None]
    lower_mask = lower_active[..., None, None]
    floating_block = own_block(floating_global)
    matrices = flexibility.reshape(local_count, 6 * face_dofs, 6 * face_dofs)

    def operate(upper_part, lower_part, offset):
        face_list = []
        for dimension in range(3):
            face_list.append(-lower_part[:, :, :, dimension])
            face_list.append(upper_part[:, :, :, dimension])
        face_loads = (
            jnp.stack(face_list, axis=3)
            .astype(jnp.bfloat16)
            .reshape(local_count, 6 * face_dofs, cases)
        )
        traces = jnp.einsum(
            "sij,sjr->sir", matrices, face_loads, preferred_element_type=jnp.float32
        )
        traces = traces.reshape(block_x, block_y, block_z, 6, face_dofs, cases)
        low_face = traces[:, :, :, 0::2]
        high_face = traces[:, :, :, 1::2] - offset
        padded_x = padded_2(
            alternate(low_face[:, :, :, 0], high_face[:, :, :, 0], 0), (("gx", 0),), 1
        )
        above_x, below_x = separate(padded_x, 0, block_x)
        padded_y = padded_2(
            alternate(low_face[:, :, :, 1], high_face[:, :, :, 1], 1), (("gy", 1),), 1
        )
        above_y, below_y = separate(padded_y, 1, block_y)
        padded_z = padded_2(
            alternate(low_face[:, :, :, 2], high_face[:, :, :, 2], 2), (("gz", 2),), 1
        )
        above_z, below_z = separate(padded_z, 2, block_z)
        upper_jump = upper_mask * (high_face - jnp.stack([above_x, above_y, above_z], axis=3))
        lower_jump = lower_mask * (jnp.stack([below_x, below_y, below_z], axis=3) - low_face)
        return (upper_jump, lower_jump)

    def coarse_solve(source):
        return jax.scipy.linalg.cho_solve(
            (factor, True), source.reshape(subdomains, cases)
        ).reshape(grid_x, grid_y, grid_z, cases)

    def correction(amplitude):
        padded = jnp.pad(amplitude, ((1, 1), (1, 1), (1, 1), (0, 0)))
        window = lax.dynamic_slice(
            padded, (start_x, start_y, start_z, 0), (block_x + 2, block_y + 2, block_z + 2, cases)
        )
        centre = window[1:-1, 1:-1, 1:-1]
        upward = [window[2:, 1:-1, 1:-1], window[1:-1, 2:, 1:-1], window[1:-1, 1:-1, 2:]]
        downward = [window[:-2, 1:-1, 1:-1], window[1:-1, :-2, 1:-1], window[1:-1, 1:-1, :-2]]
        upper_part = jnp.stack(
            [
                upper_active[..., dimension, None] * mode_value * (centre - upward[dimension])
                for dimension in range(3)
            ],
            axis=3,
        )
        lower_part = jnp.stack(
            [
                lower_active[..., dimension, None] * mode_value * (downward[dimension] - centre)
                for dimension in range(3)
            ],
            axis=3,
        )
        return (upper_part[:, :, :, :, None, :], lower_part[:, :, :, :, None, :])

    def assemble(block):
        canvas = jnp.zeros((grid_x, grid_y, grid_z, cases), jnp.float32)
        canvas = lax.dynamic_update_slice(canvas, block, (start_x, start_y, start_z, 0))
        arranged = lax.psum(canvas, ("gx", "gy", "gz"))
        return arranged

    def coarse_source(upper_part, lower_part):
        return (
            mode_value * floating_block[..., None] * jnp.sum(upper_part - lower_part, axis=(3, 4))
        )

    def inner_sums(left, right):
        return jnp.sum(left * right, axis=(0, 1, 2, 3, 4))

    def projected_norm(squared_value, source_value, amplitude_value):
        removed = jnp.sum(source_value * amplitude_value, axis=(0, 1, 2))
        removed = removed + support_value * jnp.sum(
            amplitude_value * amplitude_value, axis=(0, 1, 2)
        )
        return squared_value - removed

    def totals(stacked):
        return lax.psum(stacked, ("gx", "gy", "gz"))

    start_amplitude = coarse_solve(floating_global[..., None] * coarse_load)
    spread_upper, spread_lower = correction(start_amplitude)
    multiplier_upper = jnp.broadcast_to(spread_upper, full_shape)
    multiplier_lower = jnp.broadcast_to(spread_lower, full_shape)
    jump_upper, jump_lower = operate(multiplier_upper, multiplier_lower, dual_load)
    residual_upper = -jump_upper
    residual_lower = -jump_lower
    source = assemble(coarse_source(residual_upper, residual_lower))
    squared = totals(inner_sums(residual_upper, residual_upper)[None])[0]
    amplitude = coarse_solve(source)
    spread_upper, spread_lower = correction(amplitude)
    projected_upper = residual_upper - spread_upper
    projected_lower = residual_lower - spread_lower
    current = projected_norm(squared, source, amplitude)
    search_upper, search_lower = (projected_upper, projected_lower)
    for iteration in range(ITERS):
        applied_upper, applied_lower = operate(search_upper, search_lower, 0.0)
        partial_sums = totals(
            jnp.stack(
                [
                    inner_sums(search_upper, applied_upper),
                    inner_sums(residual_upper, applied_upper),
                    inner_sums(applied_upper, applied_upper),
                ]
            )
        )
        curvature = partial_sums[0]
        step_size = current / curvature
        multiplier_upper = multiplier_upper + step_size * search_upper
        multiplier_lower = multiplier_lower + step_size * search_lower
        residual_upper = residual_upper - step_size * applied_upper
        residual_lower = residual_lower - step_size * applied_lower
        source = assemble(coarse_source(residual_upper, residual_lower))
        amplitude = coarse_solve(source)
        spread_upper, spread_lower = correction(amplitude)
        projected_upper = residual_upper - spread_upper
        projected_lower = residual_lower - spread_lower
        squared = (
            squared - 2.0 * step_size * partial_sums[1] + step_size * step_size * partial_sums[2]
        )
        renewed = projected_norm(squared, source, amplitude)
        if iteration + 1 < ITERS:
            ratio = renewed / current
            search_upper = projected_upper + ratio * search_upper
            search_lower = projected_lower + ratio * search_lower
            current = renewed
    return (multiplier_upper, projected_upper)


def solution(mesh):
    return jax.shard_map(
        per_device,
        mesh=mesh,
        in_specs=(
            P("gx", "gy", "gz", None, None),
            P("gx", "gy", "gz", None, None, None),
            P(),
            P(),
            P(),
        ),
        out_specs=(P("gx", "gy", "gz", None, None, None), P("gx", "gy", "gz", None, None, None)),
        check_vma=False,
    )
```

profile of v0, /device:TPU:0, one launch (start us, length us, event | category | flops | bytes accessed | tf_op | source)
XLA Modules:
  0.0 567.9 jit_solution(11340886455706647938)
XLA Ops:
  3.8 5.8 %cholesky.19 = f32[64,64]{1,0:T(8,128)S(1)} custom-call(f32[64,64]{1,0:T(8,128)S(1)} %fusion.69), custom_call_target="Cholesky" | custom-call | tf_op jit(solution)/shard_map/jit(cholesky)/cholesky | solution.py:101
  18.1 6.9 %fusion.10 = f32[2,1536,128]{1,2,0:T(8,128)S(1)} fusion(bf16[2,1536,128]{2,1,0:T(8,128)(2,1)S(1)} %bitcast.457, bf16[2,1,1,1536,1536]{4,3,2,1,0:T(8,128)(2,1)} %param.7), kind=kOutput, calls=%fused_computation.10 | convolution fusion | flops 1207959552 | bytes 11796480 | tf_op jit(solution)/shard_map/sij,sjr->sir/dot_general | solution.py:135
  34.9 5.5 collective-permute-start.4
  56.1 41.0 %psum.71 = f32[4,4,4,128]{3,2,1,0:T(4,128)S(1)} all-reduce(f32[4,4,4,128]{3,2,1,0:T(4,128)S(1)} %dynamic_update_slice.15), channel_id=1, replica_groups=mesh['gx'=2,'gy'=4,'gz'=4] {'gx','gy','gz'}, use_global_device_ids=true, to_apply=%region_5.7 | all-reduce | flops 8192 | bytes 65536 | tf_op jit(solution)/shard_map/psum | solution.py:189
  98.6 6.9 %fusion.13 = f32[2,1536,128]{1,2,0:T(8,128)S(1)} fusion(bf16[2,1536,128]{2,1,0:T(8,128)(2,1)S(1)} %bitcast.458, bf16[2,1,1,1536,1536]{4,3,2,1,0:T(8,128)(2,1)} %param.7), kind=kOutput, calls=%fused_computation.11 | convolution fusion | flops 1207959552 | bytes 11796480 | tf_op jit(solution)/shard_map/sij,sjr->sir/dot_general | solution.py:135
  115.6 5.5 collective-permute-start.10
  121.7 5.3 collective-permute-start.11
  127.5 40.5 %all-reduce.15 = (f32[3,128]{1,0:T(4,128)S(1)}, f32[128]{0:T(128)S(1)}) all-reduce(f32[3,128]{1,0:T(4,128)S(1)} %pad_maximum_fusion.14, f32[128]{0:T(128)S(1)} %get-tuple-element.19), channel_id=1, replica_groups=mesh['gx'=2,'gy'=4,'gz'=4] {'gx','gy','gz'}, use_global_device_ids=true, to_apply=%region_11.13 | all-reduce | flops 512 | bytes 4096 | tf_op jit(solution)/shard_map/psum | solution.py:208
  170.9 39.8 %psum.73 = f32[4,4,4,128]{3,2,1,0:T(4,128)S(1)} all-reduce(f32[4,4,4,128]{3,2,1,0:T(4,128)S(1)} %dynamic_update_slice.16), channel_id=1, replica_groups=mesh['gx'=2,'gy'=4,'gz'=4] {'gx','gy','gz'}, use_global_device_ids=true, to_apply=%region_13.15 | all-reduce | flops 8192 | bytes 65536 | tf_op jit(solution)/shard_map/psum | solution.py:189
  214.0 8.1 %fusion.16 = f32[2,1536,128]{1,2,0:T(8,128)} fusion(bf16[2,1536,128]{2,1,0:T(8,128)(2,1)S(1)} %bitcast.460, bf16[2,1,1,1536,1536]{4,3,2,1,0:T(8,128)(2,1)} %param.7), kind=kOutput, calls=%fused_computation.12 | convolution fusion | flops 1207959552 | bytes 11796480 | tf_op jit(solution)/shard_map/sij,sjr->sir/dot_general | solution.py:135
  232.3 5.5 collective-permute-start.16
  237.8 5.3 collective-permute-start.17
  244.4 41.1 %psum.74 = f32[3,128]{1,0:T(4,128)S(1)} all-reduce(f32[3,128]{1,0:T(4,128)S(1)} %pad_maximum_fusion.15), channel_id=1, replica_groups=mesh['gx'=2,'gy'=4,'gz'=4] {'gx','gy','gz'}, use_global_device_ids=true, to_apply=%region_19.21 | all-reduce | flops 384 | bytes 3072 | tf_op jit(solution)/shard_map/psum | solution.py:208
  288.5 40.0 %psum.75 = f32[4,4,4,128]{3,2,1,0:T(4,128)S(1)} all-reduce(f32[4,4,4,128]{3,2,1,0:T(4,128)S(1)} %dynamic_update_slice.17), channel_id=1, replica_groups=mesh['gx'=2,'gy'=4,'gz'=4] {'gx','gy','gz'}, use_global_device_ids=true, to_apply=%region_21.23 | all-reduce | flops 8192 | bytes 65536 | tf_op jit(solution)/shard_map/psum | solution.py:189
  331.8 8.0 %fusion.19 = f32[2,1536,128]{1,2,0:T(8,128)} fusion(bf16[2,1536,128]{2,1,0:T(8,128)(2,1)S(1)} %bitcast.461, bf16[2,1,1,1536,1536]{4,3,2,1,0:T(8,128)(2,1)} %param.7), kind=kOutput, calls=%fused_computation.13 | convolution fusion | flops 1207959552 | bytes 11796480 | tf_op jit(solution)/shard_map/sij,sjr->sir/dot_general | solution.py:135
  351.4 5.5 collective-permute-start.22
  356.9 5.2 collective-permute-start.23
  363.7 40.4 %psum.76 = f32[3,128]{1,0:T(4,128)S(1)} all-reduce(f32[3,128]{1,0:T(4,128)S(1)} %pad_maximum_fusion.16), channel_id=1, replica_groups=mesh['gx'=2,'gy'=4,'gz'=4] {'gx','gy','gz'}, use_global_device_ids=true, to_apply=%region_27.29 | all-reduce | flops 384 | bytes 3072 | tf_op jit(solution)/shard_map/psum | solution.py:208
  407.5 39.8 %psum.77 = f32[4,4,4,128]{3,2,1,0:T(4,128)S(1)} all-reduce(f32[4,4,4,128]{3,2,1,0:T(4,128)S(1)} %dynamic_update_slice.18), channel_id=1, replica_groups=mesh['gx'=2,'gy'=4,'gz'=4] {'gx','gy','gz'}, use_global_device_ids=true, to_apply=%region_29.31 | all-reduce | flops 8192 | bytes 65536 | tf_op jit(solution)/shard_map/psum | solution.py:189
  449.8 8.1 %fusion.22 = f32[2,1536,128]{1,2,0:T(8,128)} fusion(bf16[2,1536,128]{2,1,0:T(8,128)(2,1)S(1)} %bitcast.459, bf16[2,1,1,1536,1536]{4,3,2,1,0:T(8,128)(2,1)} %param.7), kind=kOutput, calls=%fused_computation.14 | convolution fusion | flops 1207959552 | bytes 11796480 | tf_op jit(solution)/shard_map/sij,sjr->sir/dot_general | solution.py:135
  469.3 5.5 collective-permute-start.28
  474.8 5.2 collective-permute-start.29
  481.7 40.6 %psum.78 = f32[3,128]{1,0:T(4,128)S(1)} all-reduce(f32[3,128]{1,0:T(4,128)S(1)} %pad_maximum_fusion.17), channel_id=1, replica_groups=mesh['gx'=2,'gy'=4,'gz'=4] {'gx','gy','gz'}, use_global_device_ids=true, to_apply=%region_35.37 | all-reduce | flops 384 | bytes 3072 | tf_op jit(solution)/shard_map/psum | solution.py:208
  524.6 39.8 %psum.79 = f32[64,128]{1,0:T(8,128)S(1)} all-reduce(f32[64,128]{1,0:T(8,128)S(1)} %bitcast.490), channel_id=1, replica_groups=mesh['gx'=2,'gy'=4,'gz'=4] {'gx','gy','gz'}, use_global_device_ids=true, to_apply=%region_37.39 | all-reduce | flops 8192 | bytes 65536 | tf_op jit(solution)/shard_map/psum | solution.py:189
  (318 shorter events, 110.6 us)
Async XLA Ops:
  28.4 14.6 %collective-permute-start = (f32[1,1,1,256,128]{4,3,0,2,1:T(8,128)}, f32[1,1,1,256,128]{4,3,0,2,1:T(8,128)}, u32[]{:S(2)}, u32[]{:S(2)}) collective-permute-start(f32[1,1,1,256,128]{4,3,0,2,1:T(8,128)} %get-tuple-element.151), channel_id=1, source_target_pairs={{0,16},{1,17},{2,18},{3,19},{4,20},{5,21},{6,22},{7,23},{8,24},{9,... | collective-permute-start | bytes 393224 | tf_op jit(solution)/shard_map/ppermute | solution.py:18
  31.4 16.2 %collective-permute-start.1 = (f32[1,1,1,256,128]{4,3,0,2,1:T(8,128)}, f32[1,1,1,256,128]{4,3,0,2,1:T(8,128)}, u32[]{:S(2)}, u32[]{:S(2)}) collective-permute-start(f32[1,1,1,256,128]{4,3,0,2,1:T(8,128)} %get-tuple-element.152), channel_id=1, source_target_pairs={{16,0},{17,1},{18,2},{19,3},{20,4},{21,5},{22,6},{23,7},{24,8},{25... | collective-permute-start | bytes 393224 | tf_op jit(solution)/shard_map/ppermute | solution.py:20
  33.6 15.1 %collective-permute-start.2 = (f32[2,1,1,256,128]{4,3,0,2,1:T(8,128)}, f32[2,1,1,256,128]{4,3,0,2,1:T(8,128)S(1)}, u32[]{:S(2)}, u32[]{:S(2)}) collective-permute-start(f32[2,1,1,256,128]{4,3,0,2,1:T(8,128)} %get-tuple-element.148), channel_id=1, source_target_pairs={{4,0},{8,4},{12,8},{5,1},{9,5},{13,9},{6,2},{10,6},{14,10},{7,3},{... | collective-permute-start | bytes 786440 | tf_op jit(solution)/shard_map/ppermute | solution.py:20
  34.9 13.8 %collective-permute-start.4 = (f32[2,1,1,256,128]{4,3,0,2,1:T(8,128)}, f32[2,1,1,256,128]{4,3,0,2,1:T(8,128)}, u32[]{:S(2)}, u32[]{:S(2)}) collective-permute-start(f32[2,1,1,256,128]{4,3,0,2,1:T(8,128)} %get-tuple-element.147), channel_id=1, source_target_pairs={{0,4},{4,8},{8,12},{1,5},{5,9},{9,13},{2,6},{6,10},{10,14},{3,7},{... | collective-permute-start | bytes 786440 | tf_op jit(solution)/shard_map/ppermute | solution.py:18
  108.9 12.8 %collective-permute-start.6 = (f32[1,1,1,256,128]{4,3,0,2,1:T(8,128)S(1)}, f32[1,1,1,256,128]{4,3,0,2,1:T(8,128)S(1)}, u32[]{:S(2)}, u32[]{:S(2)}) collective-permute-start(f32[1,1,1,256,128]{4,3,0,2,1:T(8,128)S(1)} %get-tuple-element.145), channel_id=1, source_target_pairs={{0,16},{1,17},{2,18},{3,19},{4,20},{5,21},{6,22},{7,23},{8,24},{9,... | collective-permute-start | bytes 393224 | tf_op jit(solution)/shard_map/ppermute | solution.py:18
  110.2 16.8 %collective-permute-start.7 = (f32[1,1,1,256,128]{4,3,0,2,1:T(8,128)S(1)}, f32[1,1,1,256,128]{4,3,0,2,1:T(8,128)S(1)}, u32[]{:S(2)}, u32[]{:S(2)}) collective-permute-start(f32[1,1,1,256,128]{4,3,0,2,1:T(8,128)S(1)} %get-tuple-element.146), channel_id=1, source_target_pairs={{16,0},{17,1},{18,2},{19,3},{20,4},{21,5},{22,6},{23,7},{24,8},{25... | collective-permute-start | bytes 393224 | tf_op jit(solution)/shard_map/ppermute | solution.py:20
  112.3 14.8 %collective-permute-start.8 = (f32[2,1,1,256,128]{4,3,0,2,1:T(8,128)S(1)}, f32[2,1,1,256,128]{4,3,0,2,1:T(8,128)S(1)}, u32[]{:S(2)}, u32[]{:S(2)}) collective-permute-start(f32[2,1,1,256,128]{4,3,0,2,1:T(8,128)S(1)} %get-tuple-element.142), channel_id=1, source_target_pairs={{4,0},{8,4},{12,8},{5,1},{9,5},{13,9},{6,2},{10,6},{14,10},{7,3},{... | collective-permute-start | bytes 786440 | tf_op jit(solution)/shard_map/ppermute | solution.py:20
  114.3 12.8 %collective-permute-start.9 = (f32[2,1,1,256,128]{4,3,0,2,1:T(8,128)S(1)}, f32[2,1,1,256,128]{4,3,0,2,1:T(8,128)S(1)}, u32[]{:S(2)}, u32[]{:S(2)}) collective-permute-start(f32[2,1,1,256,128]{4,3,0,2,1:T(8,128)S(1)} %get-tuple-element.144), channel_id=1, source_target_pairs={{1,0},{2,1},{3,2},{5,4},{6,5},{7,6},{9,8},{10,9},{11,10},{13,12},{... | collective-permute-start | bytes 786440 | tf_op jit(solution)/shard_map/ppermute | solution.py:20
  115.6 52.4 %collective-permute-start.10 = (f32[2,1,1,256,128]{4,3,0,2,1:T(8,128)}, f32[2,1,1,256,128]{4,3,0,2,1:T(8,128)}, u32[]{:S(2)}, u32[]{:S(2)}) collective-permute-start(f32[2,1,1,256,128]{4,3,0,2,1:T(8,128)} %get-tuple-element.141), channel_id=1, source_target_pairs={{0,4},{4,8},{8,12},{1,5},{5,9},{9,13},{2,6},{6,10},{10,14},{3,7},{... | collective-permute-start | bytes 786440 | tf_op jit(solution)/shard_map/ppermute | solution.py:18
  121.7 46.3 %collective-permute-start.11 = (f32[2,1,1,256,128]{4,3,2,0,1:T(8,128)}, f32[2,1,1,256,128]{4,3,2,0,1:T(8,128)}, u32[]{:S(2)}, u32[]{:S(2)}) collective-permute-start(f32[2,1,1,256,128]{4,3,2,0,1:T(8,128)} %get-tuple-element.143), channel_id=1, source_target_pairs={{0,1},{1,2},{2,3},{4,5},{5,6},{6,7},{8,9},{9,10},{10,11},{12,13},{... | collective-permute-start | bytes 786440 | tf_op jit(solution)/shard_map/ppermute | solution.py:18
  227.4 15.7 %collective-permute-start.13 = (f32[1,1,1,256,128]{4,3,0,2,1:T(8,128)S(1)}, f32[1,1,1,256,128]{4,3,0,2,1:T(8,128)S(1)}, u32[]{:S(2)}, u32[]{:S(2)}) collective-permute-start(f32[1,1,1,256,128]{4,3,0,2,1:T(8,128)S(1)} %get-tuple-element.140), channel_id=1, source_target_pairs={{16,0},{17,1},{18,2},{19,3},{20,4},{21,5},{22,6},{23,7},{24,8},{25... | collective-permute-start | bytes 393224 | tf_op jit(solution)/shard_map/ppermute | solution.py:20
  229.5 13.7 %collective-permute-start.14 = (f32[2,1,1,256,128]{4,3,0,1,2:T(8,128)S(1)}, f32[2,1,1,256,128]{4,3,0,1,2:T(8,128)S(1)}, u32[]{:S(2)}, u32[]{:S(2)}) collective-permute-start(f32[2,1,1,256,128]{4,3,0,1,2:T(8,128)S(1)} %get-tuple-element.135), channel_id=1, source_target_pairs={{4,0},{8,4},{12,8},{5,1},{9,5},{13,9},{6,2},{10,6},{14,10},{7,3},{... | collective-permute-start | bytes 786440 | tf_op jit(solution)/shard_map/ppermute | solution.py:20
  232.3 53.2 %collective-permute-start.16 = (f32[2,1,1,256,128]{4,3,0,1,2:T(8,128)}, f32[2,1,1,256,128]{4,3,0,1,2:T(8,128)}, u32[]{:S(2)}, u32[]{:S(2)}) collective-permute-start(f32[2,1,1,256,128]{4,3,0,1,2:T(8,128)} %get-tuple-element.136), channel_id=1, source_target_pairs={{0,4},{4,8},{8,12},{1,5},{5,9},{9,13},{2,6},{6,10},{10,14},{3,7},{... | collective-permute-start | bytes 786440 | tf_op jit(solution)/shard_map/ppermute | solution.py:18
  237.8 47.7 %collective-permute-start.17 = (f32[2,1,1,256,128]{4,3,0,2,1:T(8,128)S(1)}, f32[2,1,1,256,128]{4,3,0,2,1:T(8,128)}, u32[]{:S(2)}, u32[]{:S(2)}) collective-permute-start(f32[2,1,1,256,128]{4,3,0,2,1:T(8,128)S(1)} %get-tuple-element.138), channel_id=1, source_target_pairs={{0,1},{1,2},{2,3},{4,5},{5,6},{6,7},{8,9},{9,10},{10,11},{12,13},{... | collective-permute-start | bytes 786440 | tf_op jit(solution)/shard_map/ppermute | solution.py:18
  345.9 16.2 %collective-permute-start.19 = (f32[1,1,1,256,128]{4,3,0,2,1:T(8,128)S(1)}, f32[1,1,1,256,128]{4,3,0,2,1:T(8,128)S(1)}, u32[]{:S(2)}, u32[]{:S(2)}) collective-permute-start(f32[1,1,1,256,128]{4,3,0,2,1:T(8,128)S(1)} %get-tuple-element.134), channel_id=1, source_target_pairs={{16,0},{17,1},{18,2},{19,3},{20,4},{21,5},{22,6},{23,7},{24,8},{25... | collective-permute-start | bytes 393224 | tf_op jit(solution)/shard_map/ppermute | solution.py:20
  348.0 14.9 %collective-permute-start.20 = (f32[2,1,1,256,128]{4,3,0,2,1:T(8,128)S(1)}, f32[2,1,1,256,128]{4,3,0,2,1:T(8,128)S(1)}, u32[]{:S(2)}, u32[]{:S(2)}) collective-permute-start(f32[2,1,1,256,128]{4,3,0,2,1:T(8,128)S(1)} %get-tuple-element.129), channel_id=1, source_target_pairs={{4,0},{8,4},{12,8},{5,1},{9,5},{13,9},{6,2},{10,6},{14,10},{7,3},{... | collective-permute-start | bytes 786440 | tf_op jit(solution)/shard_map/ppermute | solution.py:20
  350.1 12.9 %collective-permute-start.21 = (f32[2,1,1,256,128]{4,3,0,2,1:T(8,128)S(1)}, f32[2,1,1,256,128]{4,3,0,2,1:T(8,128)S(1)}, u32[]{:S(2)}, u32[]{:S(2)}) collective-permute-start(f32[2,1,1,256,128]{4,3,0,2,1:T(8,128)S(1)} %get-tuple-element.131), channel_id=1, source_target_pairs={{1,0},{2,1},{3,2},{5,4},{6,5},{7,6},{9,8},{10,9},{11,10},{13,12},{... | collective-permute-start | bytes 786440 | tf_op jit(solution)/shard_map/ppermute | solution.py:20
  351.4 52.8 %collective-permute-start.22 = (f32[2,1,1,256,128]{4,3,0,2,1:T(8,128)}, f32[2,1,1,256,128]{4,3,0,2,1:T(8,128)}, u32[]{:S(2)}, u32[]{:S(2)}) collective-permute-start(f32[2,1,1,256,128]{4,3,0,2,1:T(8,128)} %get-tuple-element.130), channel_id=1, source_target_pairs={{0,4},{4,8},{8,12},{1,5},{5,9},{9,13},{2,6},{6,10},{10,14},{3,7},{... | collective-permute-start | bytes 786440 | tf_op jit(solution)/shard_map/ppermute | solution.py:18
  356.9 47.3 %collective-permute-start.23 = (f32[2,1,1,256,128]{4,3,2,0,1:T(8,128)}, f32[2,1,1,256,128]{4,3,2,0,1:T(8,128)}, u32[]{:S(2)}, u32[]{:S(2)}) collective-permute-start(f32[2,1,1,256,128]{4,3,2,0,1:T(8,128)} %get-tuple-element.132), channel_id=1, source_target_pairs={{0,1},{1,2},{2,3},{4,5},{5,6},{6,7},{8,9},{9,10},{10,11},{12,13},{... | collective-permute-start | bytes 786440 | tf_op jit(solution)/shard_map/ppermute | solution.py:18
  463.9 16.2 %collective-permute-start.25 = (f32[1,1,1,256,128]{4,3,0,2,1:T(8,128)S(1)}, f32[1,1,1,256,128]{4,3,0,2,1:T(8,128)S(1)}, u32[]{:S(2)}, u32[]{:S(2)}) collective-permute-start(f32[1,1,1,256,128]{4,3,0,2,1:T(8,128)S(1)} %get-tuple-element.128), channel_id=1, source_target_pairs={{16,0},{17,1},{18,2},{19,3},{20,4},{21,5},{22,6},{23,7},{24,8},{25... | collective-permute-start | bytes 393224 | tf_op jit(solution)/shard_map/ppermute | solution.py:20
  466.0 14.9 %collective-permute-start.26 = (f32[2,1,1,256,128]{4,3,0,2,1:T(8,128)S(1)}, f32[2,1,1,256,128]{4,3,0,2,1:T(8,128)S(1)}, u32[]{:S(2)}, u32[]{:S(2)}) collective-permute-start(f32[2,1,1,256,128]{4,3,0,2,1:T(8,128)S(1)} %get-tuple-element.124), channel_id=1, source_target_pairs={{4,0},{8,4},{12,8},{5,1},{9,5},{13,9},{6,2},{10,6},{14,10},{7,3},{... | collective-permute-start | bytes 786440 | tf_op jit(solution)/shard_map/ppermute | solution.py:20
  468.0 12.9 %collective-permute-start.27 = (f32[2,1,1,256,128]{4,3,0,2,1:T(8,128)S(1)}, f32[2,1,1,256,128]{4,3,0,2,1:T(8,128)S(1)}, u32[]{:S(2)}, u32[]{:S(2)}) collective-permute-start(f32[2,1,1,256,128]{4,3,0,2,1:T(8,128)S(1)} %get-tuple-element.126), channel_id=1, source_target_pairs={{1,0},{2,1},{3,2},{5,4},{6,5},{7,6},{9,8},{10,9},{11,10},{13,12},{... | collective-permute-start | bytes 786440 | tf_op jit(solution)/shard_map/ppermute | solution.py:20
  469.3 53.0 %collective-permute-start.28 = (f32[2,1,1,256,128]{4,3,0,2,1:T(8,128)}, f32[2,1,1,256,128]{4,3,0,2,1:T(8,128)}, u32[]{:S(2)}, u32[]{:S(2)}) collective-permute-start(f32[2,1,1,256,128]{4,3,0,2,1:T(8,128)} %get-tuple-element.123), channel_id=1, source_target_pairs={{0,4},{4,8},{8,12},{1,5},{5,9},{9,13},{2,6},{6,10},{10,14},{3,7},{... | collective-permute-start | bytes 786440 | tf_op jit(solution)/shard_map/ppermute | solution.py:18
  474.8 47.5 %collective-permute-start.29 = (f32[2,1,1,256,128]{4,3,2,0,1:T(8,128)}, f32[2,1,1,256,128]{4,3,2,0,1:T(8,128)}, u32[]{:S(2)}, u32[]{:S(2)}) collective-permute-start(f32[2,1,1,256,128]{4,3,2,0,1:T(8,128)} %get-tuple-element.125), channel_id=1, source_target_pairs={{0,1},{1,2},{2,3},{4,5},{5,6},{6,7},{8,9},{9,10},{10,11},{12,13},{... | collective-permute-start | bytes 786440 | tf_op jit(solution)/shard_map/ppermute | solution.py:18
  (29 other events, 597.4 us)
where the time goes:
time: 570 us; the launch traced here: 568 us
  blocking collectives  363 us (64%)
  starting transfers between devices  80.8 us (14%)
  other arithmetic  43.5 us (8%)
  matrix products  40.9 us (7%)
  local copies, waits for them, and re-layouts  32 us (6%)
  waiting for transfers between devices  5.72 us (1%)
    psum x5, blocking collectives, assemble(): arranged = lax.psum(canvas, ('gx', 'gy', 'gz'))  200 us
    psum x4, blocking collectives, totals(): return lax.psum(stacked, ('gx', 'gy', 'gz'))  163 us
    ppermute x15, starting transfers between devices, padded_2(): lax.ppermute(tail, axis, [(i, (i + 1) % count) for i in range(ends)])  61.4 us
    dot_general x5, matrix products, operate(): jnp.einsum('sij,sjr->sir', matrices, face_loads, preferred_element_type=j...  37.9 us
    ppermute x15, starting transfers between devices, padded_2(): lax.ppermute(head, axis, [((i + 1) % count, i) for i in range(ends)])  19.4 us
    reduce_sum x5, other arithmetic, coarse_source(): jnp.sum(upper_part - lower_part, axis=(3, 4))  12.7 us
  transfers between devices with their start and end apart: 30, of which 2 were waited for; matrix products, arithmetic and copies ran while one was open for 2% of the time, Pallas kernels for 0%

commit v1 on v0

--- a/solution.py
+++ b/solution.py
@@ -186,7 +186,7 @@
     def assemble(block):
         canvas = jnp.zeros((grid_x, grid_y, grid_z, cases), jnp.float32)
         canvas = lax.dynamic_update_slice(canvas, block, (start_x, start_y, start_z, 0))
-        arranged = lax.psum(canvas, ("gx", "gy", "gz"))
+        arranged = lax.psum(lax.psum(canvas, ("gy", "gz")), "gx")
         return arranged
 
     def coarse_source(upper_part, lower_part):

time: 570 us -> 759 us (1.33)
  blocking collectives: 363 us -> 549 us
    psum x5 -> x10, blocking collectives: 200 us -> 395 us  [assemble(): arranged = lax.psum(lax.psum(canvas, ('gy', 'gz')), 'gx')]
    psum x4, blocking collectives: 163 us -> 154 us  [totals(): return lax.psum(stacked, ('gx', 'gy', 'gz'))]
where the time goes in v1:
time: 759 us; the launch traced here: 756 us
  blocking collectives  549 us (72%)
  starting transfers between devices  83.6 us (11%)
  other arithmetic  43.5 us (6%)
  matrix products  40.9 us (5%)
  local copies, waits for them, and re-layouts  32 us (4%)
    psum x10, blocking collectives, assemble(): arranged = lax.psum(lax.psum(canvas, ('gy', 'gz')), 'gx')  395 us
    psum x4, blocking collectives, totals(): return lax.psum(stacked, ('gx', 'gy', 'gz'))  154 us
    ppermute x15, starting transfers between devices, padded_2(): lax.ppermute(tail, axis, [(i, (i + 1) % count) for i in range(ends)])  64.2 us
    dot_general x5, matrix products, operate(): jnp.einsum('sij,sjr->sir', matrices, face_loads, preferred_element_type=j...  37.9 us
    ppermute x15, starting transfers between devices, padded_2(): lax.ppermute(head, axis, [((i + 1) % count, i) for i in range(ends)])  19.4 us
  transfers between devices with their start and end apart: 30, of which 2 were waited for; matrix products, arithmetic and copies ran while one was open for 2% of the time, Pallas kernels for 0%

profile of v1, /device:TPU:0, one launch (start us, length us, event | category | flops | bytes accessed | tf_op | source)
XLA Modules:
  0.0 756.5 jit_solution(518189441359054895)
XLA Ops:
  3.8 5.8 cholesky.19
  18.1 6.9 fusion.10
  34.9 5.5 collective-permute-start.4
  56.1 76.0 %psum.106 = f32[4,4,4,128]{3,2,1,0:T(4,128)S(1)} all-reduce(f32[4,4,4,128]{3,2,1,0:T(4,128)S(1)} %dynamic_update_slice.15), channel_id=1, replica_groups=mesh['gx'=2,'gy'=4,'gz'=4] {'gy','gz'}, use_global_device_ids=true, to_apply=%region_5.7 | all-reduce | flops 8192 | bytes 65536 | tf_op jit(solution)/shard_map/psum | solution.py:189
  137.0 6.9 fusion.13
  154.9 5.3 collective-permute-start.10
  160.7 5.3 collective-permute-start.11
  166.6 39.9 %all-reduce.15 = (f32[3,128]{1,0:T(4,128)S(1)}, f32[128]{0:T(128)S(1)}) all-reduce(f32[3,128]{1,0:T(4,128)S(1)} %pad_maximum_fusion.14, f32[128]{0:T(128)S(1)} %get-tuple-element.19), channel_id=1, replica_groups=mesh['gx'=2,'gy'=4,'gz'=4] {'gx','gy','gz'}, use_global_device_ids=true, to_apply=%region_12.14 | all-reduce | flops 512 | bytes 4096 | tf_op jit(solution)/shard_map/psum | solution.py:208
  209.4 75.3 %psum.109 = f32[4,4,4,128]{3,2,1,0:T(4,128)S(1)} all-reduce(f32[4,4,4,128]{3,2,1,0:T(4,128)S(1)} %dynamic_update_slice.16), channel_id=1, replica_groups=mesh['gx'=2,'gy'=4,'gz'=4] {'gy','gz'}, use_global_device_ids=true, to_apply=%region_14.16 | all-reduce | flops 8192 | bytes 65536 | tf_op jit(solution)/shard_map/psum | solution.py:189
  291.4 8.0 %fusion.16 = f32[2,1536,128]{1,2,0:T(8,128)} fusion(bf16[2,1536,128]{2,1,0:T(8,128)(2,1)S(1)} %bitcast.460, bf16[2,1,1,1536,1536]{4,3,2,1,0:T(8,128)(2,1)} %param.7), kind=kOutput, calls=%fused_computation.12 | convolution fusion | flops 1207959552 | bytes 11796480 | tf_op jit(solution)/shard_map/sij,sjr->sir/dot_general | solution.py:135
  310.7 5.2 collective-permute-start.16
  315.9 5.3 collective-permute-start.17
  322.5 38.6 %psum.111 = f32[3,128]{1,0:T(4,128)S(1)} all-reduce(f32[3,128]{1,0:T(4,128)S(1)} %pad_maximum_fusion.15), channel_id=1, replica_groups=mesh['gx'=2,'gy'=4,'gz'=4] {'gx','gy','gz'}, use_global_device_ids=true, to_apply=%region_21.23 | all-reduce | flops 384 | bytes 3072 | tf_op jit(solution)/shard_map/psum | solution.py:208
  364.2 75.3 %psum.112 = f32[4,4,4,128]{3,2,1,0:T(4,128)S(1)} all-reduce(f32[4,4,4,128]{3,2,1,0:T(4,128)S(1)} %dynamic_update_slice.17), channel_id=1, replica_groups=mesh['gx'=2,'gy'=4,'gz'=4] {'gy','gz'}, use_global_device_ids=true, to_apply=%region_23.25 | all-reduce | flops 8192 | bytes 65536 | tf_op jit(solution)/shard_map/psum | solution.py:189
  446.2 8.0 %fusion.19 = f32[2,1536,128]{1,2,0:T(8,128)} fusion(bf16[2,1536,128]{2,1,0:T(8,128)(2,1)S(1)} %bitcast.461, bf16[2,1,1,1536,1536]{4,3,2,1,0:T(8,128)(2,1)} %param.7), kind=kOutput, calls=%fused_computation.13 | convolution fusion | flops 1207959552 | bytes 11796480 | tf_op jit(solution)/shard_map/sij,sjr->sir/dot_general | solution.py:135
  466.7 5.3 collective-permute-start.22
  471.9 5.2 collective-permute-start.23
  478.8 37.8 %psum.114 = f32[3,128]{1,0:T(4,128)S(1)} all-reduce(f32[3,128]{1,0:T(4,128)S(1)} %pad_maximum_fusion.16), channel_id=1, replica_groups=mesh['gx'=2,'gy'=4,'gz'=4] {'gx','gy','gz'}, use_global_device_ids=true, to_apply=%region_30.32 | all-reduce | flops 384 | bytes 3072 | tf_op jit(solution)/shard_map/psum | solution.py:208
  520.0 75.6 %psum.115 = f32[4,4,4,128]{3,2,1,0:T(4,128)S(1)} all-reduce(f32[4,4,4,128]{3,2,1,0:T(4,128)S(1)} %dynamic_update_slice.18), channel_id=1, replica_groups=mesh['gx'=2,'gy'=4,'gz'=4] {'gy','gz'}, use_global_device_ids=true, to_apply=%region_32.34 | all-reduce | flops 8192 | bytes 65536 | tf_op jit(solution)/shard_map/psum | solution.py:189
  601.5 8.1 %fusion.22 = f32[2,1536,128]{1,2,0:T(8,128)} fusion(bf16[2,1536,128]{2,1,0:T(8,128)(2,1)S(1)} %bitcast.459, bf16[2,1,1,1536,1536]{4,3,2,1,0:T(8,128)(2,1)} %param.7), kind=kOutput, calls=%fused_computation.14 | convolution fusion | flops 1207959552 | bytes 11796480 | tf_op jit(solution)/shard_map/sij,sjr->sir/dot_general | solution.py:135
  622.0 5.3 collective-permute-start.28
  627.2 5.2 collective-permute-start.29
  634.1 37.5 %psum.117 = f32[3,128]{1,0:T(4,128)S(1)} all-reduce(f32[3,128]{1,0:T(4,128)S(1)} %pad_maximum_fusion.17), channel_id=1, replica_groups=mesh['gx'=2,'gy'=4,'gz'=4] {'gx','gy','gz'}, use_global_device_ids=true, to_apply=%region_39.41 | all-reduce | flops 384 | bytes 3072 | tf_op jit(solution)/shard_map/psum | solution.py:208
  673.9 75.6 %psum.118 = f32[4,4,4,128]{3,2,1,0:T(4,128)S(1)} all-reduce(f32[4,4,4,128]{3,2,1,0:T(4,128)S(1)} %dynamic_update_slice.19), channel_id=1, replica_groups=mesh['gx'=2,'gy'=4,'gz'=4] {'gy','gz'}, use_global_device_ids=true, to_apply=%region_41.43 | all-reduce | flops 8192 | bytes 65536 | tf_op jit(solution)/shard_map/psum | solution.py:189
  (323 shorter events, 131.3 us)
Async XLA Ops:
  28.4 14.6 %collective-permute-start = (f32[1,1,1,256,128]{4,3,0,2,1:T(8,128)}, f32[1,1,1,256,128]{4,3,0,2,1:T(8,128)}, u32[]{:S(2)}, u32[]{:S(2)}) collective-permute-start(f32[1,1,1,256,128]{4,3,0,2,1:T(8,128)} %get-tuple-element.151), channel_id=1, source_target_pairs={{0,16},{1,17},{2,18},{3,19},{4,20},{5,21},{6,22},{7,23},{8,24},{9,... | collective-permute-start | bytes 393224 | tf_op jit(solution)/shard_map/ppermute | solution.py:18
  31.4 16.2 %collective-permute-start.1 = (f32[1,1,1,256,128]{4,3,0,2,1:T(8,128)}, f32[1,1,1,256,128]{4,3,0,2,1:T(8,128)}, u32[]{:S(2)}, u32[]{:S(2)}) collective-permute-start(f32[1,1,1,256,128]{4,3,0,2,1:T(8,128)} %get-tuple-element.152), channel_id=1, source_target_pairs={{16,0},{17,1},{18,2},{19,3},{20,4},{21,5},{22,6},{23,7},{24,8},{25... | collective-permute-start | bytes 393224 | tf_op jit(solution)/shard_map/ppermute | solution.py:20
  33.6 15.1 %collective-permute-start.2 = (f32[2,1,1,256,128]{4,3,0,2,1:T(8,128)}, f32[2,1,1,256,128]{4,3,0,2,1:T(8,128)S(1)}, u32[]{:S(2)}, u32[]{:S(2)}) collective-permute-start(f32[2,1,1,256,128]{4,3,0,2,1:T(8,128)} %get-tuple-element.148), channel_id=1, source_target_pairs={{4,0},{8,4},{12,8},{5,1},{9,5},{13,9},{6,2},{10,6},{14,10},{7,3},{... | collective-permute-start | bytes 786440 | tf_op jit(solution)/shard_map/ppermute | solution.py:20
  34.9 13.8 %collective-permute-start.4 = (f32[2,1,1,256,128]{4,3,0,2,1:T(8,128)}, f32[2,1,1,256,128]{4,3,0,2,1:T(8,128)}, u32[]{:S(2)}, u32[]{:S(2)}) collective-permute-start(f32[2,1,1,256,128]{4,3,0,2,1:T(8,128)} %get-tuple-element.147), channel_id=1, source_target_pairs={{0,4},{4,8},{8,12},{1,5},{5,9},{9,13},{2,6},{6,10},{10,14},{3,7},{... | collective-permute-start | bytes 786440 | tf_op jit(solution)/shard_map/ppermute | solution.py:18
  147.2 13.5 %collective-permute-start.6 = (f32[1,1,1,256,128]{4,3,0,2,1:T(8,128)S(1)}, f32[1,1,1,256,128]{4,3,0,2,1:T(8,128)S(1)}, u32[]{:S(2)}, u32[]{:S(2)}) collective-permute-start(f32[1,1,1,256,128]{4,3,0,2,1:T(8,128)S(1)} %get-tuple-element.145), channel_id=1, source_target_pairs={{0,16},{1,17},{2,18},{3,19},{4,20},{5,21},{6,22},{7,23},{8,24},{9,... | collective-permute-start | bytes 393224 | tf_op jit(solution)/shard_map/ppermute | solution.py:18
  149.5 16.5 %collective-permute-start.7 = (f32[1,1,1,256,128]{4,3,0,2,1:T(8,128)S(1)}, f32[1,1,1,256,128]{4,3,0,2,1:T(8,128)S(1)}, u32[]{:S(2)}, u32[]{:S(2)}) collective-permute-start(f32[1,1,1,256,128]{4,3,0,2,1:T(8,128)S(1)} %get-tuple-element.146), channel_id=1, source_target_pairs={{16,0},{17,1},{18,2},{19,3},{20,4},{21,5},{22,6},{23,7},{24,8},{25... | collective-permute-start | bytes 393224 | tf_op jit(solution)/shard_map/ppermute | solution.py:20
  151.6 14.6 %collective-permute-start.8 = (f32[2,1,1,256,128]{4,3,0,2,1:T(8,128)S(1)}, f32[2,1,1,256,128]{4,3,0,2,1:T(8,128)S(1)}, u32[]{:S(2)}, u32[]{:S(2)}) collective-permute-start(f32[2,1,1,256,128]{4,3,0,2,1:T(8,128)S(1)} %get-tuple-element.142), channel_id=1, source_target_pairs={{4,0},{8,4},{12,8},{5,1},{9,5},{13,9},{6,2},{10,6},{14,10},{7,3},{... | collective-permute-start | bytes 786440 | tf_op jit(solution)/shard_map/ppermute | solution.py:20
  154.9 51.6 %collective-permute-start.10 = (f32[2,1,1,256,128]{4,3,0,2,1:T(8,128)}, f32[2,1,1,256,128]{4,3,0,2,1:T(8,128)}, u32[]{:S(2)}, u32[]{:S(2)}) collective-permute-start(f32[2,1,1,256,128]{4,3,0,2,1:T(8,128)} %get-tuple-element.141), channel_id=1, source_target_pairs={{0,4},{4,8},{8,12},{1,5},{5,9},{9,13},{2,6},{6,10},{10,14},{3,7},{... | collective-permute-start | bytes 786440 | tf_op jit(solution)/shard_map/ppermute | solution.py:18
  160.7 45.8 %collective-permute-start.11 = (f32[2,1,1,256,128]{4,3,2,0,1:T(8,128)}, f32[2,1,1,256,128]{4,3,2,0,1:T(8,128)}, u32[]{:S(2)}, u32[]{:S(2)}) collective-permute-start(f32[2,1,1,256,128]{4,3,2,0,1:T(8,128)} %get-tuple-element.143), channel_id=1, source_target_pairs={{0,1},{1,2},{2,3},{4,5},{5,6},{6,7},{8,9},{9,10},{10,11},{12,13},{... | collective-permute-start | bytes 786440 | tf_op jit(solution)/shard_map/ppermute | solution.py:18
  305.8 15.4 %collective-permute-start.13 = (f32[1,1,1,256,128]{4,3,0,2,1:T(8,128)S(1)}, f32[1,1,1,256,128]{4,3,0,2,1:T(8,128)S(1)}, u32[]{:S(2)}, u32[]{:S(2)}) collective-permute-start(f32[1,1,1,256,128]{4,3,0,2,1:T(8,128)S(1)} %get-tuple-element.140), channel_id=1, source_target_pairs={{16,0},{17,1},{18,2},{19,3},{20,4},{21,5},{22,6},{23,7},{24,8},{25... | collective-permute-start | bytes 393224 | tf_op jit(solution)/shard_map/ppermute | solution.py:20
  307.9 13.4 %collective-permute-start.14 = (f32[2,1,1,256,128]{4,3,0,1,2:T(8,128)S(1)}, f32[2,1,1,256,128]{4,3,0,1,2:T(8,128)S(1)}, u32[]{:S(2)}, u32[]{:S(2)}) collective-permute-start(f32[2,1,1,256,128]{4,3,0,1,2:T(8,128)S(1)} %get-tuple-element.135), channel_id=1, source_target_pairs={{4,0},{8,4},{12,8},{5,1},{9,5},{13,9},{6,2},{10,6},{14,10},{7,3},{... | collective-permute-start | bytes 786440 | tf_op jit(solution)/shard_map/ppermute | solution.py:20
  310.7 50.4 %collective-permute-start.16 = (f32[2,1,1,256,128]{4,3,0,1,2:T(8,128)}, f32[2,1,1,256,128]{4,3,0,1,2:T(8,128)}, u32[]{:S(2)}, u32[]{:S(2)}) collective-permute-start(f32[2,1,1,256,128]{4,3,0,1,2:T(8,128)} %get-tuple-element.136), channel_id=1, source_target_pairs={{0,4},{4,8},{8,12},{1,5},{5,9},{9,13},{2,6},{6,10},{10,14},{3,7},{... | collective-permute-start | bytes 786440 | tf_op jit(solution)/shard_map/ppermute | solution.py:18
  315.9 45.2 %collective-permute-start.17 = (f32[2,1,1,256,128]{4,3,0,2,1:T(8,128)S(1)}, f32[2,1,1,256,128]{4,3,0,2,1:T(8,128)}, u32[]{:S(2)}, u32[]{:S(2)}) collective-permute-start(f32[2,1,1,256,128]{4,3,0,2,1:T(8,128)S(1)} %get-tuple-element.138), channel_id=1, source_target_pairs={{0,1},{1,2},{2,3},{4,5},{5,6},{6,7},{8,9},{9,10},{10,11},{12,13},{... | collective-permute-start | bytes 786440 | tf_op jit(solution)/shard_map/ppermute | solution.py:18
  459.0 13.0 %collective-permute-start.18 = (f32[1,1,1,256,128]{4,3,0,2,1:T(8,128)S(1)}, f32[1,1,1,256,128]{4,3,0,2,1:T(8,128)S(1)}, u32[]{:S(2)}, u32[]{:S(2)}) collective-permute-start(f32[1,1,1,256,128]{4,3,0,2,1:T(8,128)S(1)} %get-tuple-element.133), channel_id=1, source_target_pairs={{0,16},{1,17},{2,18},{3,19},{4,20},{5,21},{6,22},{7,23},{8,24},{9,... | collective-permute-start | bytes 393224 | tf_op jit(solution)/shard_map/ppermute | solution.py:18
  461.2 16.0 %collective-permute-start.19 = (f32[1,1,1,256,128]{4,3,0,2,1:T(8,128)S(1)}, f32[1,1,1,256,128]{4,3,0,2,1:T(8,128)S(1)}, u32[]{:S(2)}, u32[]{:S(2)}) collective-permute-start(f32[1,1,1,256,128]{4,3,0,2,1:T(8,128)S(1)} %get-tuple-element.134), channel_id=1, source_target_pairs={{16,0},{17,1},{18,2},{19,3},{20,4},{21,5},{22,6},{23,7},{24,8},{25... | collective-permute-start | bytes 393224 | tf_op jit(solution)/shard_map/ppermute | solution.py:20
  463.3 14.7 %collective-permute-start.20 = (f32[2,1,1,256,128]{4,3,0,2,1:T(8,128)S(1)}, f32[2,1,1,256,128]{4,3,0,2,1:T(8,128)S(1)}, u32[]{:S(2)}, u32[]{:S(2)}) collective-permute-start(f32[2,1,1,256,128]{4,3,0,2,1:T(8,128)S(1)} %get-tuple-element.129), channel_id=1, source_target_pairs={{4,0},{8,4},{12,8},{5,1},{9,5},{13,9},{6,2},{10,6},{14,10},{7,3},{... | collective-permute-start | bytes 786440 | tf_op jit(solution)/shard_map/ppermute | solution.py:20
  466.7 50.0 %collective-permute-start.22 = (f32[2,1,1,256,128]{4,3,0,2,1:T(8,128)}, f32[2,1,1,256,128]{4,3,0,2,1:T(8,128)}, u32[]{:S(2)}, u32[]{:S(2)}) collective-permute-start(f32[2,1,1,256,128]{4,3,0,2,1:T(8,128)} %get-tuple-element.130), channel_id=1, source_target_pairs={{0,4},{4,8},{8,12},{1,5},{5,9},{9,13},{2,6},{6,10},{10,14},{3,7},{... | collective-permute-start | bytes 786440 | tf_op jit(solution)/shard_map/ppermute | solution.py:18
  471.9 44.7 %collective-permute-start.23 = (f32[2,1,1,256,128]{4,3,2,0,1:T(8,128)}, f32[2,1,1,256,128]{4,3,2,0,1:T(8,128)}, u32[]{:S(2)}, u32[]{:S(2)}) collective-permute-start(f32[2,1,1,256,128]{4,3,2,0,1:T(8,128)} %get-tuple-element.132), channel_id=1, source_target_pairs={{0,1},{1,2},{2,3},{4,5},{5,6},{6,7},{8,9},{9,10},{10,11},{12,13},{... | collective-permute-start | bytes 786440 | tf_op jit(solution)/shard_map/ppermute | solution.py:18
  614.3 13.0 %collective-permute-start.24 = (f32[1,1,1,256,128]{4,3,0,2,1:T(8,128)S(1)}, f32[1,1,1,256,128]{4,3,0,2,1:T(8,128)S(1)}, u32[]{:S(2)}, u32[]{:S(2)}) collective-permute-start(f32[1,1,1,256,128]{4,3,0,2,1:T(8,128)S(1)} %get-tuple-element.127), channel_id=1, source_target_pairs={{0,16},{1,17},{2,18},{3,19},{4,20},{5,21},{6,22},{7,23},{8,24},{9,... | collective-permute-start | bytes 393224 | tf_op jit(solution)/shard_map/ppermute | solution.py:18
  616.5 16.0 %collective-permute-start.25 = (f32[1,1,1,256,128]{4,3,0,2,1:T(8,128)S(1)}, f32[1,1,1,256,128]{4,3,0,2,1:T(8,128)S(1)}, u32[]{:S(2)}, u32[]{:S(2)}) collective-permute-start(f32[1,1,1,256,128]{4,3,0,2,1:T(8,128)S(1)} %get-tuple-element.128), channel_id=1, source_target_pairs={{16,0},{17,1},{18,2},{19,3},{20,4},{21,5},{22,6},{23,7},{24,8},{25... | collective-permute-start | bytes 393224 | tf_op jit(solution)/shard_map/ppermute | solution.py:20
  618.6 14.7 %collective-permute-start.26 = (f32[2,1,1,256,128]{4,3,0,2,1:T(8,128)S(1)}, f32[2,1,1,256,128]{4,3,0,2,1:T(8,128)S(1)}, u32[]{:S(2)}, u32[]{:S(2)}) collective-permute-start(f32[2,1,1,256,128]{4,3,0,2,1:T(8,128)S(1)} %get-tuple-element.124), channel_id=1, source_target_pairs={{4,0},{8,4},{12,8},{5,1},{9,5},{13,9},{6,2},{10,6},{14,10},{7,3},{... | collective-permute-start | bytes 786440 | tf_op jit(solution)/shard_map/ppermute | solution.py:20
  620.7 12.6 %collective-permute-start.27 = (f32[2,1,1,256,128]{4,3,0,2,1:T(8,128)S(1)}, f32[2,1,1,256,128]{4,3,0,2,1:T(8,128)S(1)}, u32[]{:S(2)}, u32[]{:S(2)}) collective-permute-start(f32[2,1,1,256,128]{4,3,0,2,1:T(8,128)S(1)} %get-tuple-element.126), channel_id=1, source_target_pairs={{1,0},{2,1},{3,2},{5,4},{6,5},{7,6},{9,8},{10,9},{11,10},{13,12},{... | collective-permute-start | bytes 786440 | tf_op jit(solution)/shard_map/ppermute | solution.py:20
  622.0 49.7 %collective-permute-start.28 = (f32[2,1,1,256,128]{4,3,0,2,1:T(8,128)}, f32[2,1,1,256,128]{4,3,0,2,1:T(8,128)}, u32[]{:S(2)}, u32[]{:S(2)}) collective-permute-start(f32[2,1,1,256,128]{4,3,0,2,1:T(8,128)} %get-tuple-element.123), channel_id=1, source_target_pairs={{0,4},{4,8},{8,12},{1,5},{5,9},{9,13},{2,6},{6,10},{10,14},{3,7},{... | collective-permute-start | bytes 786440 | tf_op jit(solution)/shard_map/ppermute | solution.py:18
  627.2 44.4 %collective-permute-start.29 = (f32[2,1,1,256,128]{4,3,2,0,1:T(8,128)}, f32[2,1,1,256,128]{4,3,2,0,1:T(8,128)}, u32[]{:S(2)}, u32[]{:S(2)}) collective-permute-start(f32[2,1,1,256,128]{4,3,2,0,1:T(8,128)} %get-tuple-element.125), channel_id=1, source_target_pairs={{0,1},{1,2},{2,3},{4,5},{5,6},{6,7},{8,9},{9,10},{10,11},{12,13},{... | collective-permute-start | bytes 786440 | tf_op jit(solution)/shard_map/ppermute | solution.py:18
  (29 other events, 868.6 us)
